TPU v7x, 32 devices: a whole 2x2x4 slice. The times are simulated.
32 devices in a mesh: row: 4 (over x, core), col: 8 (over z, y).
Axes of the slice: x: 2, y: 2, z: 4, core: 2. Of those that a mesh axis runs over, the one named last changes fastest.
Arguments:
- front_panels: float32 [16, 4, 256, 8, 8, 256], P(None, 'row', 'col'), as said below
- child_update_tiles: float32 [4, 8, 8, 256, 256], P('row', 'col'), may hold values from -2 to 2
- child_rows: int32 [4, 8, 8], P('row', 'col'), may hold values from 0 to 63, as said below
- child_cols: int32 [4, 8, 8], P('row', 'col'), may hold values from 0 to 7
- child_counts: int32 [4, 8], P('row', 'col'), may hold values from 4 to 8, as said below
- row_maps: int32 [4, 8, 8, 256], P('row', 'col'), may hold values from 0 to 255, each once within a row
- col_maps: int32 [4, 8, 8, 256], P('row', 'col'), may hold values from 0 to 255, each once within a row
Outputs:
- factored_front: float32 [16, 4, 256, 8, 8, 256], P(None, 'row', None, None, 'col')
Inputs may be any that keep to these rules, and one draw needn't show every extreme that they name: child_rows[r, c, k] modulo 4 names one of four owner rows; among the live slots of one device at most 2 name the same owner row, and some device sends exactly 2 to some owner; every slot's target tile column is at most its target tile row. `child_counts`: every device of col index 0 has all slots live. `front_panels`: the diagonal of the front dominates its first tile, so that tile stays positive definite after the children are added.
All inputs are finite; a program needn't handle non-finite values.
Results may differ from a plain program's by a relative error of at most 0.0003.
Values sent between devices are 32-bit elements; how exact they have to be, the bound alone decides.
No kernel may reach another device: no remote copies, remote signals or barrier semaphores. Data moves between devices by JAX's collectives and lax.ppermute only.
A program may use at most 320 MiB of HBM per device.

v0:
```python
import jax
import jax.numpy as jnp
from jax import lax
from jax.sharding import PartitionSpec as P


def broadcast(value, axis, source):
    kept = jnp.where(lax.axis_index(axis) == source, value, 0).astype(value.dtype)
    return lax.psum(kept, axis)


def slot_positions(owners, is_live):
    slot_entries = owners.shape[-1]
    earlier = lax.broadcasted_iota(
        jnp.int32, (slot_entries, slot_entries), 0
    ) < lax.broadcasted_iota(jnp.int32, (slot_entries, slot_entries), 1)
    same_owner = (owners[..., :, None] == owners[..., None, :]) & is_live[..., :, None] & earlier
    return jnp.sum(same_owner.astype(jnp.int32), axis=-2)


def on_device(
    front_panels, child_update_tiles, child_rows, child_cols, child_counts, row_maps, col_maps
):
    largest_index = lax.Precision.HIGHEST
    row_size = lax.axis_size("row")
    col_size = lax.axis_size("col")
    my_row = lax.axis_index("row")
    my_col = lax.axis_index("col")
    front_width = front_panels.shape[-1]
    blocks = lax.all_to_all(front_panels, "col", split_axis=4, concat_axis=2, tiled=True)
    row_tiles = blocks.shape[0]
    col_tiles = blocks.shape[3]
    blocks = blocks.reshape(row_tiles, front_width, col_tiles, front_width)
    slot_entries = child_update_tiles.shape[2]
    capacity = slot_entries // 4
    labels = lax.broadcasted_iota(jnp.int32, (1, 1, front_width), 2)
    row_indicator = (row_maps.reshape(slot_entries, front_width)[:, :, None] == labels).astype(
        jnp.float32
    )
    column_indicator = (col_maps.reshape(slot_entries, front_width)[:, :, None] == labels).astype(
        jnp.float32
    )
    shifted_tiles = jnp.einsum(
        "gml,gmq->glq",
        row_indicator,
        child_update_tiles.reshape(slot_entries, front_width, front_width),
        precision=largest_index,
    )
    shifted_tiles = jnp.einsum(
        "afb,abx->afx", shifted_tiles, column_indicator, precision=largest_index
    )
    slot_ids = lax.broadcasted_iota(jnp.int32, (slot_entries,), 0)
    is_live = slot_ids < child_counts.reshape(())
    owners = child_rows.reshape(slot_entries) % row_size
    positions = slot_positions(owners, is_live)
    dest_ids = lax.broadcasted_iota(jnp.int32, (row_size, capacity, slot_entries), 0)
    place_ids = lax.broadcasted_iota(jnp.int32, (row_size, capacity, slot_entries), 1)
    selector = (
        (owners[None, None, :] == dest_ids)
        & (positions[None, None, :] == place_ids)
        & is_live[None, None, :]
    ).astype(jnp.float32)
    outgoing = jnp.einsum(
        "opk,kx->opx",
        selector,
        shifted_tiles.reshape(slot_entries, front_width * front_width),
        precision=largest_index,
    )
    incoming = lax.all_to_all(outgoing, "row", split_axis=0, concat_axis=0, tiled=True)
    all_rows, all_cols, all_counts = (
        lax.all_gather(child_rows, "row", axis=0, tiled=True),
        lax.all_gather(child_cols, "row", axis=0, tiled=True),
        lax.all_gather(child_counts, "row", axis=0, tiled=True),
    )
    source_rows = all_rows.reshape(row_size, slot_entries)
    source_cols = all_cols.reshape(row_size, slot_entries)
    source_live = slot_ids[None, :] < all_counts.reshape(row_size)[:, None]
    source_owner = source_rows % row_size
    source_pos = slot_positions(source_owner, source_live)
    mine = (source_live & (source_owner == my_row)).astype(jnp.float32)
    depth_onehot = (
        (source_rows // row_size)[:, :, None]
        == lax.broadcasted_iota(jnp.int32, (1, 1, row_tiles), 2)
    ).astype(jnp.float32) * mine[:, :, None]
    across_onehot = (
        source_cols[:, :, None] == lax.broadcasted_iota(jnp.int32, (1, 1, col_tiles), 2)
    ).astype(jnp.float32)
    place_onehot = (
        source_pos[:, :, None] == lax.broadcasted_iota(jnp.int32, (1, 1, capacity), 2)
    ).astype(jnp.float32)
    landing = jnp.einsum(
        "ska,skb,skp->absp", depth_onehot, across_onehot, place_onehot, precision=largest_index
    )
    incoming = incoming.reshape(row_size, capacity, front_width, front_width)
    blocks = blocks + jnp.einsum("absp,spxy->axby", landing, incoming, precision=largest_index)
    tile_i = lax.broadcasted_iota(jnp.int32, (row_tiles, 1, col_tiles, 1), 0) * row_size + my_row
    tile_j = lax.broadcasted_iota(jnp.int32, (row_tiles, 1, col_tiles, 1), 2) * col_size + my_col
    flipped = jnp.einsum("axby->aybx", blocks)
    blocks = jnp.where(tile_i == tile_j, 0.5 * (blocks + flipped), blocks)
    identity = jnp.eye(front_width, dtype=jnp.float32)
    corner = blocks[0, :, 0, :]
    at_root = (my_row == 0) & (my_col == 0)
    factor = jnp.linalg.cholesky(jnp.where(at_root, corner, identity))
    factor = broadcast(factor, "row", 0)
    column = blocks[:, :, 0, :].reshape(row_tiles * front_width, front_width)
    solved = jax.scipy.linalg.solve_triangular(factor, column.T, lower=True).T.reshape(
        row_tiles, front_width, front_width
    )
    tile_index = lax.broadcasted_iota(jnp.int32, (row_tiles, 1, 1), 0) * row_size + my_row
    kept = jnp.where(tile_index == 0, factor[None, :, :], solved)
    below = jnp.where(tile_index == 0, 0.0, solved)
    row_panel = broadcast(below, "col", 0)
    group = col_size // row_size
    whole = lax.all_gather(row_panel, "row", axis=0, tiled=True)
    whole = whole.reshape(row_size, col_tiles, group, front_width, front_width)
    picked = lax.dynamic_index_in_dim(whole, my_col % row_size, 0, keepdims=False)
    col_panel = lax.dynamic_index_in_dim(picked, my_col // row_size, 1, keepdims=False)
    blocks = blocks - jnp.einsum("asx,bqx->asbq", row_panel, col_panel, precision=largest_index)
    first_column = jnp.where(my_col == 0, kept, blocks[:, :, 0, :])
    blocks = blocks.at[:, :, 0, :].set(first_column)
    blocks = jnp.where(tile_i >= tile_j, blocks, 0.0)
    return blocks.reshape(row_tiles, 1, front_width, col_tiles, 1, front_width)


def solution(mesh):
    return jax.shard_map(
        on_device,
        mesh=mesh,
        in_specs=(
            P(None, "row", "col", None, None, None),
            P("row", "col", None, None, None),
            P("row", "col", None),
            P("row", "col", None),
            P("row", "col"),
            P("row", "col", None, None),
            P("row", "col", None, None),
        ),
        out_specs=P(None, "row", None, None, "col", None),
        check_vma=False,
    )
```

profile of v0, /device:TPU:0, one launch (start us, length us, event | category | flops | bytes accessed | tf_op | source)
XLA Modules:
  0.0 1470.2 jit_solution(9605571834959242759)
XLA Ops:
  6.5 0.8 and_select_fusion.1
  8.1 2.2 fusion.8
  10.3 2.6 fusion.11
  13.0 2.0 reshape.354
  15.7 4.1 fusion.33
  19.8 4.2 all-to-all-start.1
  24.0 30.6 %copy.67 = f32[16,1,32,8,8,256]{5,3,2,0,1,4:T(8,128)} copy(f32[16,1,32,8,8,256]{5,4,3,2,1,0:T(8,128)} %param.9) | data formatting | bytes 67108864 | tf_op args[0]
  54.6 1.3 copy-done.4
  55.9 7.1 all-to-all-start
  64.2 5.8 all-reduce.1
  70.0 5.0 all_gather.14
  75.0 5.2 all_gather.17
  81.3 3.5 reshape.323
  84.8 30.9 %convolution_bitcast_fusion = f32[256,256,16,8]{1,2,3,0:T(8,128)} fusion(f32[4,2,256,256,1]{3,2,1,0,4:T(8,128)S(1)} %bitcast.110, f32[16,8,4,2]{0,1,3,2:T(8,128)S(1)} %convolution_bitcast_fusion.1), kind=kOutput, calls=%fused_computation.8 | convolution fusion | flops 805306368 | bytes 35655680 | tf_op jit(solution)/shard_map/absp,spxy->axby/dot_general | solution.py:95
  115.7 34.4 %copy.72 = f32[256,256,16,8]{0,1,3,2:T(8,128)} copy(f32[256,256,16,8]{1,2,3,0:T(8,128)} %convolution_bitcast_fusion) | data formatting | bytes 67108864 | tf_op jit(solution)/shard_map/absp,spxy->axby/dot_general | solution.py:95
  150.2 637.7 %all-to-all-done = f32[16,1,32,8,8,256]{5,3,2,0,1,4:T(8,128)} async-done(((f32[16,1,32,8,8,256]{5,3,2,0,1,4:T(8,128)}), f32[16,1,32,8,8,256]{5,3,2,0,1,4:T(8,128)}, u32[]{:S(2)}, u32[]{:S(2)}) %all-to-all-start) | async-done | bytes 33554464 | tf_op jit(solution)/shard_map/all_to_all | solution.py:30
  787.9 22.9 %copy.68 = f32[16,1,32,8,8,256]{5,3,2,4,0,1:T(8,128)} copy(f32[16,1,32,8,8,256]{5,3,2,0,1,4:T(8,128)} %all-to-all-done) | data formatting | bytes 67108864 | tf_op jit(solution)/shard_map/all_to_all | solution.py:30
  810.7 35.0 %copy.73 = f32[16,256,8,256]{1,3,2,0:T(8,128)} copy(f32[16,256,8,256]{3,2,1,0:T(8,128)} %bitcast.104) | data formatting | bytes 67108864 | tf_op jit(solution)/shard_map/reshape | solution.py:33
  845.7 33.5 %bitcast_add_fusion.1 = f32[16,256,8,256]{1,3,2,0:T(8,128)} fusion(f32[16,256,8,256]{1,3,2,0:T(8,128)} %copy.73, f32[256,256,16,8]{0,1,3,2:T(8,128)} %copy.72), kind=kLoop, calls=%fused_computation.5 | loop fusion | flops 8388608 | bytes 100663296 | tf_op jit(solution)/shard_map/add | solution.py:95
  879.2 31.9 %copy.74 = f32[16,256,8,256]{3,1,2,0:T(8,128)} copy(f32[16,256,8,256]{1,3,2,0:T(8,128)} %bitcast_add_fusion.1) | data formatting | bytes 67108864 | tf_op jit(solution)/shard_map/add | solution.py:95
  911.2 33.6 %fusion.1 = f32[16,256,8,256]{1,3,2,0:T(8,128)} fusion(f32[16,256,8,256]{1,3,2,0:T(8,128)} %bitcast_add_fusion.1, f32[16,256,8,256]{3,1,2,0:T(8,128)} %copy.74, pred[16,8]{1,0:T(8,128)(4,1)S(1)} %get-tuple-element.42), kind=kLoop, calls=%fused_computation.4 | loop fusion | flops 25165824 | bytes 100663424 | tf_op jit(solution)/shard_map/jit(_where)/select_n | solution.py:99
  944.8 1.0 fusion.14
  945.9 1.0 fusion.15
  947.0 11.7 cholesky.50
  958.7 9.8 custom-call.15
  969.0 11.7 cholesky.105
  983.6 4.5 slice.96
  988.1 5.8 copy.76
  993.9 5.7 copy.77
  999.6 14.6 all-reduce.5.cloned.1.call-done
  1014.1 1.0 fusion.16
  1015.2 3.9 while.2
  1015.8 1.3 bitcast_dynamic-update-slice_fusion.3
  1017.7 1.3 bitcast_dynamic-update-slice_fusion.3
  1019.0 19.7 %custom-call.16 = f32[2,128,128]{1,2,0:T(8,128)S(1)} custom-call(f32[2,128,128]{2,1,0:T(8,128)S(1)} %get-tuple-element.24), custom_call_target="InvertDiagBlocksLowerTriangular" | custom-call | tf_op jit(solution)/shard_map/jit(_solve_triangular)/triangular_solve | solution.py:106
  1038.7 3.6 fusion.4
  1042.4 1.9 convolution_subtract_fusion.1
  1044.3 1.9 fusion.18
  1046.3 2.4 maximum_bitcast_fusion
  1048.6 5.6 copy.94
  1054.2 4.7 select_select_fusion
  1059.0 156.4 %all-reduce.7.cloned.1.call-done = f32[16,256,256]{2,1,0:T(8,128)} async-done(((f32[16,256,256]{2,1,0:T(8,128)}), f32[16,256,256]{2,1,0:T(8,128)}) %all-reduce.7.cloned.1.call-update) | async-done | bytes 4194320 | tf_op jit(solution)/shard_map/psum | solution.py:9
  1215.5 5.6 copy.83
  1221.2 100.9 %all-gather.2.cloned.1.call-done = f32[64,256,256]{2,1,0:T(8,128)} async-done(((f32[16,256,256]{2,1,0:T(8,128)}), f32[64,256,256]{2,1,0:T(8,128)}) %all-gather.2.cloned.1.call-update) | async-done | bytes 16777232 | tf_op jit(solution)/shard_map/all_gather | solution.py:114
  1322.0 35.3 %convolution_subtract_fusion = f32[16,256,8,256]{1,3,2,0:T(8,128)} fusion(f32[16,256,8,256]{1,3,2,0:T(8,128)} %fusion.1, f32[16,256,256]{2,1,0:T(8,128)} %all-reduce.7.cloned.1.call-done, f32[4,8,2,256,256]{4,3,2,1,0:T(8,128)} %bitcast.111, s32[]{:T(128)S(6)} %select_n.139, s32[]{:T(128)S(6)} %select_n.142), kind=kOutput, calls=%fused_computation.7 | convolution fusion | flops 25778192384 | bytes 73400328 | tf_op jit(solution)/shard_map/asx,bqx->asbq/dot_general | solution.py:118
  1357.3 4.8 fusion.2
  1362.2 22.9 %select_bitcast_fusion = f32[16,1,256,8,1,256]{2,5,3,0,4,1:T(8,128)} fusion(f32[16,256,8,256]{1,3,2,0:T(8,128)} %fusion.2, pred[16,8]{1,0:T(8,128)(4,1)S(1)} %copy-done.6), kind=kLoop, calls=%fused_computation.6 | loop fusion | flops 8388608 | bytes 67108992 | tf_op jit(solution)/shard_map/reshape | solution.py:122
  1385.1 78.3 %copy.84 = f32[16,1,256,8,1,256]{5,4,3,2,1,0:T(1,128)} copy(f32[16,1,256,8,1,256]{2,5,3,0,4,1:T(8,128)} %select_bitcast_fusion) | data formatting | bytes 67108864 | tf_op jit(solution)/shard_map/reshape | solution.py:122
  (64 shorter events, 6.9 us)
Async XLA Ops:
  6.5 1.6 copy-start
  6.5 3.8 copy-start.7
  19.8 34.8 %all-to-all-start.1 = ((f32[4,2,65536]{2,1,0:T(2,128)}), f32[4,2,65536]{2,1,0:T(2,128)S(1)}, u32[]{:S(2)}, u32[]{:S(2)}) async-start(f32[4,2,65536]{2,1,0:T(2,128)} %fusion.33), calls=%async_computation.1 | async-start | bytes 4194304 | tf_op jit(solution)/shard_map/all_to_all | solution.py:69
  54.6 8.5 copy-start.10
  54.6 15.4 %copy-start.8 = (s32[1,1,8]{2,1,0:T(1,128)S(1)}, s32[1,1,8]{2,1,0:T(1,128)}, u32[]{:S(2)}) copy-start(s32[1,1,8]{2,1,0:T(1,128)} %param.11) | copy-start | bytes 100
  54.6 20.5 %copy-start.9 = (s32[1,1,8]{2,1,0:T(1,128)S(1)}, s32[1,1,8]{2,1,0:T(1,128)}, u32[]{:S(2)}) copy-start(s32[1,1,8]{2,1,0:T(1,128)} %param.12) | copy-start | bytes 100
  54.6 1.3 copy-start.4
  55.9 731.9 %all-to-all-start = ((f32[16,1,32,8,8,256]{5,3,2,0,1,4:T(8,128)}), f32[16,1,32,8,8,256]{5,3,2,0,1,4:T(8,128)}, u32[]{:S(2)}, u32[]{:S(2)}) async-start(f32[16,1,32,8,8,256]{5,3,2,0,1,4:T(8,128)} %copy.67), calls=%async_computation | async-start | bytes 67108864 | tf_op jit(solution)/shard_map/all_to_all | solution.py:30
  63.0 951.1 %all-reduce.5.cloned.1.call-start = ((), (), s32[]{:S(2)}) async-start(), calls=%async_computation.2 | async-start | bytes 524288 | tf_op jit(solution)/shard_map/psum | solution.py:9
  983.5 231.9 %all-reduce.7.cloned.1.call-start = ((), (), s32[]{:S(2)}) async-start(), calls=%async_computation.3 | async-start | bytes 8388608 | tf_op jit(solution)/shard_map/psum | solution.py:9
  1038.7 3.7 copy-start.3
  1059.0 263.1 %all-gather.2.cloned.1.call-start = ((), (), s32[]{:S(2)}) async-start(), calls=%async_computation.4 | async-start | bytes 20971520 | tf_op jit(solution)/shard_map/all_gather | solution.py:114
  1215.5 5.6 copy-start.5
  1322.0 35.3 %copy-start.2 = (f32[16,256,1,256]{1,3,2,0:T(8,128)S(1)}, f32[16,256,1,256]{1,3,2,0:T(8,128)}, u32[]{:S(2)}) copy-start(f32[16,256,1,256]{1,3,2,0:T(8,128)} %copy.83) | copy-start | bytes 12582916
  1357.3 4.8 copy-start.6
  1385.1 78.3 %copy-start.1 = (f32[1,1,8,256,256]{4,3,2,1,0:T(8,128)S(1)}, f32[1,1,8,256,256]{4,3,2,1,0:T(8,128)}, u32[]{:S(2)}) copy-start(f32[1,1,8,256,256]{4,3,2,1,0:T(8,128)} %param.10) | copy-start | bytes 6291460
Sparse Core Ops, SparseCore 0:
  983.6 30.4 all-reduce.4
  1059.1 156.2 all-reduce.6
  1217.1 104.9 all-gather.1
where the time goes:
time: 1480 us; the launch traced here: 1470 us
  waiting for transfers between devices  910 us (61%)
  local copies, waits for them, and re-layouts  273 us (18%)
  other arithmetic  162 us (11%)
  matrix products  83.3 us (6%)
  blocking collectives  16 us (1%)
  between operations  15.5 us (1%)
    all_to_all x1, waiting for transfers between devices, on_device(): lax.all_to_all(front_panels, 'col', split_axis=4, concat_axis=2, tiled=True)  638 us
    psum x2, waiting for transfers between devices, broadcast(): return lax.psum(kept, axis)  171 us
    all_gather x1, waiting for transfers between devices, on_device(): whole = lax.all_gather(row_panel, 'row', axis=0, tiled=True)  101 us
    reshape x1, local copies, waits for them, and re-layouts, on_device(): return blocks.reshape(row_tiles, 1, front_width, col_tiles, 1, front_width)  78.3 us
    dot_general x1, matrix products, on_device(): jnp.einsum('asx,bqx->asbq', row_panel, col_panel, precision=largest_index)  35.3 us
    reshape x1, local copies, waits for them, and re-layouts, on_device(): blocks = blocks.reshape(row_tiles, front_width, col_tiles, front_width)  35 us
    dot_general x1, local copies, waits for them, and re-layouts, on_device(): jnp.einsum('absp,spxy->axby', landing, incoming, precision=largest_index)  34.4 us
    another operation x6, other arithmetic, on_device(): factor = jnp.linalg.cholesky(jnp.where(at_root, corner, identity))  34 us
  transfers between devices with their start and end apart: 5, of which 4 were waited for; matrix products, arithmetic and copies ran while one was open for 8% of the time, Pallas kernels for 0%

commit v1 on v0

--- a/solution.py
+++ b/solution.py
@@ -2,6 +2,28 @@
 import jax.numpy as jnp
 from jax import lax
 from jax.sharding import PartitionSpec as P
+
+
+def joined_along(blocks, dim):
+    blocks = jnp.moveaxis(blocks, 0, dim)
+    lengths = blocks.shape
+    return blocks.reshape(*lengths[:dim], lengths[dim] * lengths[dim + 1], *lengths[dim + 2 :])
+
+
+def ring_gather(value, axis, dim):
+    size = lax.axis_size(axis)
+    pairs = [(i, (i + 1) % size) for i in range(size)]
+    back = [(b, a) for a, b in pairs]
+    lower, upper = ([], [])
+    for turn in range(size - 1):
+        if turn % 2 == 0:
+            lower.append(lax.ppermute(lower[-1] if lower else value, axis, pairs))
+        else:
+            upper.append(lax.ppermute(upper[-1] if upper else value, axis, back))
+    pieces = jnp.stack([*lower[::-1], value, *upper])
+    shift = lax.axis_index(axis) - len(lower)
+    pieces = pieces[(jnp.arange(size) - shift) % size]
+    return joined_along(pieces, dim)
 
 
 def broadcast(value, axis, source):
@@ -111,7 +133,7 @@
     below = jnp.where(tile_index == 0, 0.0, solved)
     row_panel = broadcast(below, "col", 0)
     group = col_size // row_size
-    whole = lax.all_gather(row_panel, "row", axis=0, tiled=True)
+    whole = ring_gather(row_panel, "row", 0)
     whole = whole.reshape(row_size, col_tiles, group, front_width, front_width)
     picked = lax.dynamic_index_in_dim(whole, my_col % row_size, 0, keepdims=False)
     col_panel = lax.dynamic_index_in_dim(picked, my_col // row_size, 1, keepdims=False)

time: 1480 us -> 1550 us (1.047)
  waiting for transfers between devices: 910 us -> 941 us
  local copies, waits for them, and re-layouts: 273 us -> 294 us
  other arithmetic: 162 us -> 180 us
    ppermute x0 -> x3, waiting for transfers between devices: none -> 132 us  [the longest x2 132 us: ring_gather(): lower.append(lax.ppermute(lower[-1] if lower else value, axis, pairs))]
    all_gather x1 -> x0, waiting for transfers between devices: 101 us -> none  [on_device(): whole = lax.all_gather(row_panel, 'row', axis=0, tiled=True)]
    gather x0 -> x3, local copies, waits for them, and re-layouts: none -> 21.6 us  [ring_gather(): pieces = pieces[(jnp.arange(size) - shift) % size]]
    unnamed x26 -> x28, local copies, waits for them, and re-layouts: 33.2 us -> 33.4 us
  transfers between devices with their start and end apart: 5 -> 7, of which waited for: 4 -> 5; matrix products, arithmetic and copies ran while one was open for 8% -> 8% of each run, Pallas kernels for 0% -> 0%
where the time goes in v1:
time: 1550 us; the launch traced here: 1540 us
  waiting for transfers between devices  941 us (61%)
  local copies, waits for them, and re-layouts  294 us (19%)
  other arithmetic  180 us (12%)
  matrix products  82.8 us (5%)
  blocking collectives  16 us (1%)
  between operations  15.9 us (1%)
    all_to_all x1, waiting for transfers between devices, on_device(): lax.all_to_all(front_panels, 'col', split_axis=4, concat_axis=2, tiled=True)  638 us
    psum x2, waiting for transfers between devices, broadcast(): return lax.psum(kept, axis)  171 us
    ppermute x2, waiting for transfers between devices, ring_gather(): lower.append(lax.ppermute(lower[-1] if lower else value, axis, pairs))  132 us
    reshape x1, local copies, waits for them, and re-layouts, on_device(): return blocks.reshape(row_tiles, 1, front_width, col_tiles, 1, front_width)  78.3 us
    reshape x1, local copies, waits for them, and re-layouts, on_device(): blocks = blocks.reshape(row_tiles, front_width, col_tiles, front_width)  35 us
    dot_general x1, matrix products, on_device(): jnp.einsum('asx,bqx->asbq', row_panel, col_panel, precision=largest_index)  34.9 us
    dot_general x1, local copies, waits for them, and re-layouts, on_device(): jnp.einsum('absp,spxy->axby', landing, incoming, precision=largest_index)  34.4 us
    another operation x6, other arithmetic, on_device(): factor = jnp.linalg.cholesky(jnp.where(at_root, corner, identity))  34 us
  transfers between devices with their start and end apart: 7, of which 5 were waited for; matrix products, arithmetic and copies ran while one was open for 8% of the time, Pallas kernels for 0%

profile of v1, /device:TPU:0, one launch (start us, length us, event | category | flops | bytes accessed | tf_op | source)
XLA Modules:
  0.0 1543.1 jit_solution(7049445988811103189)
XLA Ops:
  8.1 2.2 fusion.8
  10.3 2.6 fusion.11
  13.0 2.0 reshape.415
  15.7 4.1 fusion.33
  19.8 4.2 all-to-all-start.1
  24.0 30.6 %copy.67 = f32[16,1,32,8,8,256]{5,3,2,0,1,4:T(8,128)} copy(f32[16,1,32,8,8,256]{5,4,3,2,1,0:T(8,128)} %param.9) | data formatting | bytes 67108864 | tf_op args[0]
  55.9 7.1 all-to-all-start
  64.4 5.8 all-reduce.1
  70.2 5.0 all_gather.11
  75.2 5.2 all_gather.14
  81.5 3.5 reshape.369
  85.0 30.9 %convolution_bitcast_fusion = f32[256,256,16,8]{1,2,3,0:T(8,128)} fusion(f32[4,2,256,256,1]{3,2,1,0,4:T(8,128)S(1)} %bitcast.118, f32[16,8,4,2]{0,1,3,2:T(8,128)S(1)} %convolution_bitcast_fusion.1), kind=kOutput, calls=%fused_computation.12 | convolution fusion | flops 805306368 | bytes 35655680 | tf_op jit(solution)/shard_map/absp,spxy->axby/dot_general | solution.py:117
  115.9 34.4 %copy.72 = f32[256,256,16,8]{0,1,3,2:T(8,128)} copy(f32[256,256,16,8]{1,2,3,0:T(8,128)} %convolution_bitcast_fusion) | data formatting | bytes 67108864 | tf_op jit(solution)/shard_map/absp,spxy->axby/dot_general | solution.py:117
  150.3 637.5 %all-to-all-done = f32[16,1,32,8,8,256]{5,3,2,0,1,4:T(8,128)} async-done(((f32[16,1,32,8,8,256]{5,3,2,0,1,4:T(8,128)}), f32[16,1,32,8,8,256]{5,3,2,0,1,4:T(8,128)}, u32[]{:S(2)}, u32[]{:S(2)}) %all-to-all-start) | async-done | bytes 33554464 | tf_op jit(solution)/shard_map/all_to_all | solution.py:52
  787.9 22.9 %copy.68 = f32[16,1,32,8,8,256]{5,3,2,4,0,1:T(8,128)} copy(f32[16,1,32,8,8,256]{5,3,2,0,1,4:T(8,128)} %all-to-all-done) | data formatting | bytes 67108864 | tf_op jit(solution)/shard_map/all_to_all | solution.py:52
  810.7 35.0 %copy.73 = f32[16,256,8,256]{1,3,2,0:T(8,128)} copy(f32[16,256,8,256]{3,2,1,0:T(8,128)} %bitcast.110) | data formatting | bytes 67108864 | tf_op jit(solution)/shard_map/reshape | solution.py:55
  845.7 33.5 %bitcast_add_fusion.1 = f32[16,256,8,256]{1,3,2,0:T(8,128)} fusion(f32[16,256,8,256]{1,3,2,0:T(8,128)} %copy.73, f32[256,256,16,8]{0,1,3,2:T(8,128)} %copy.72), kind=kLoop, calls=%fused_computation.7 | loop fusion | flops 8388608 | bytes 100663296 | tf_op jit(solution)/shard_map/add | solution.py:117
  879.2 32.0 %copy.74 = f32[16,256,8,256]{3,1,2,0:T(8,128)} copy(f32[16,256,8,256]{1,3,2,0:T(8,128)} %bitcast_add_fusion.1) | data formatting | bytes 67108864 | tf_op jit(solution)/shard_map/add | solution.py:117
  911.3 33.6 %fusion.1 = f32[16,256,8,256]{1,3,2,0:T(8,128)} fusion(f32[16,256,8,256]{1,3,2,0:T(8,128)} %bitcast_add_fusion.1, f32[16,256,8,256]{3,1,2,0:T(8,128)} %copy.74, pred[16,8]{1,0:T(8,128)(4,1)S(1)} %get-tuple-element.44), kind=kLoop, calls=%fused_computation.6 | loop fusion | flops 25165824 | bytes 100663424 | tf_op jit(solution)/shard_map/jit(_where)/select_n | solution.py:121
  947.0 11.7 cholesky.50
  958.8 9.8 custom-call.15
  969.1 11.7 cholesky.105
  983.7 4.5 slice.100
  988.3 5.8 copy.76
  994.1 5.7 copy.77
  999.7 14.5 all-reduce.5.cloned.1.call-done
  1015.3 3.8 while.2
  1019.1 19.7 %custom-call.16 = f32[2,128,128]{1,2,0:T(8,128)S(1)} custom-call(f32[2,128,128]{2,1,0:T(8,128)S(1)} %get-tuple-element.24), custom_call_target="InvertDiagBlocksLowerTriangular" | custom-call | tf_op jit(solution)/shard_map/jit(_solve_triangular)/triangular_solve | solution.py:128
  1038.8 3.6 fusion.4
  1042.4 1.9 convolution_subtract_fusion.1
  1044.4 1.9 fusion.18
  1046.3 2.4 maximum_bitcast_fusion
  1048.7 5.6 copy.94
  1054.3 4.7 select_select_fusion
  1059.1 156.5 %all-reduce.7.cloned.1.call-done = f32[16,256,256]{2,1,0:T(8,128)} async-done(((f32[16,256,256]{2,1,0:T(8,128)}), f32[16,256,256]{2,1,0:T(8,128)}) %all-reduce.7.cloned.1.call-update) | async-done | bytes 4194320 | tf_op jit(solution)/shard_map/psum | solution.py:31
  1215.6 1.7 collective-permute-start.2
  1217.3 89.6 %collective-permute-done = f32[16,256,256]{2,1,0:T(8,128)} collective-permute-done((f32[16,256,256]{2,1,0:T(8,128)}, f32[16,256,256]{2,1,0:T(8,128)}, u32[]{:S(2)}, u32[]{:S(2)}) %collective-permute-start) | collective-permute-done | bytes 4194336 | tf_op jit(solution)/shard_map/ppermute | solution.py:20
  1307.0 5.5 copy.83
  1312.7 42.4 %collective-permute-done.1 = f32[16,256,256]{2,1,0:T(8,128)} collective-permute-done((f32[16,256,256]{2,1,0:T(8,128)}, f32[16,256,256]{2,1,0:T(8,128)}, u32[]{:S(2)}, u32[]{:S(2)}) %collective-permute-start.1) | collective-permute-done | bytes 4194336 | tf_op jit(solution)/shard_map/ppermute | solution.py:20
  1355.2 6.5 pad_maximum_fusion
  1361.7 6.3 fusion.47
  1368.0 7.7 gather_fusion.1
  1375.6 7.7 gather_fusion
  1383.3 11.8 pad_maximum_fusion.1
  1395.1 34.9 %convolution_subtract_fusion = f32[16,256,8,256]{1,3,2,0:T(8,128)} fusion(f32[16,256,8,256]{1,3,2,0:T(8,128)} %fusion.1, f32[16,256,256]{2,1,0:T(8,128)S(1)} %copy-done.4, f32[4,8,2,256,256]{4,3,2,1,0:T(8,128)} %bitcast.113, s32[]{:T(128)S(6)} %select_n.164, s32[]{:T(128)S(6)} %select_n.167), kind=kOutput, calls=%fused_computation.11 | convolution fusion | flops 25778192384 | bytes 73400328 | tf_op jit(solution)/shard_map/asx,bqx->asbq/dot_general | solution.py:140
  1430.0 4.8 fusion.2
  1434.8 22.9 %select_bitcast_fusion = f32[16,1,256,8,1,256]{2,5,3,0,4,1:T(8,128)} fusion(f32[16,256,8,256]{1,3,2,0:T(8,128)} %fusion.2, pred[16,8]{1,0:T(8,128)(4,1)S(1)} %copy-done.7), kind=kLoop, calls=%fused_computation.8 | loop fusion | flops 8388608 | bytes 67108992 | tf_op jit(solution)/shard_map/reshape | solution.py:144
  1457.8 78.3 %copy.84 = f32[16,1,256,8,1,256]{5,4,3,2,1,0:T(1,128)} copy(f32[16,1,256,8,1,256]{2,5,3,0,4,1:T(8,128)} %select_bitcast_fusion) | data formatting | bytes 67108864 | tf_op jit(solution)/shard_map/reshape | solution.py:144
  (76 shorter events, 14.7 us)
Async XLA Ops:
  6.5 1.6 copy-start
  6.5 3.8 copy-start.8
  19.8 34.8 %all-to-all-start.1 = ((f32[4,2,65536]{2,1,0:T(2,128)}), f32[4,2,65536]{2,1,0:T(2,128)S(1)}, u32[]{:S(2)}, u32[]{:S(2)}) async-start(f32[4,2,65536]{2,1,0:T(2,128)} %fusion.33), calls=%async_computation.1 | async-start | bytes 4194304 | tf_op jit(solution)/shard_map/all_to_all | solution.py:91
  54.6 8.5 copy-start.11
  54.6 15.6 %copy-start.9 = (s32[1,1,8]{2,1,0:T(1,128)S(1)}, s32[1,1,8]{2,1,0:T(1,128)}, u32[]{:S(2)}) copy-start(s32[1,1,8]{2,1,0:T(1,128)} %param.11) | copy-start | bytes 100
  54.6 20.6 %copy-start.10 = (s32[1,1,8]{2,1,0:T(1,128)S(1)}, s32[1,1,8]{2,1,0:T(1,128)}, u32[]{:S(2)}) copy-start(s32[1,1,8]{2,1,0:T(1,128)} %param.12) | copy-start | bytes 100
  54.6 1.4 copy-start.5
  55.9 731.9 %all-to-all-start = ((f32[16,1,32,8,8,256]{5,3,2,0,1,4:T(8,128)}), f32[16,1,32,8,8,256]{5,3,2,0,1,4:T(8,128)}, u32[]{:S(2)}, u32[]{:S(2)}) async-start(f32[16,1,32,8,8,256]{5,3,2,0,1,4:T(8,128)} %copy.67), calls=%async_computation | async-start | bytes 67108864 | tf_op jit(solution)/shard_map/all_to_all | solution.py:52
  63.0 951.2 %all-reduce.5.cloned.1.call-start = ((), (), s32[]{:S(2)}) async-start(), calls=%async_computation.2 | async-start | bytes 524288 | tf_op jit(solution)/shard_map/psum | solution.py:31
  983.7 231.9 %all-reduce.7.cloned.1.call-start = ((), (), s32[]{:S(2)}) async-start(), calls=%async_computation.3 | async-start | bytes 8388608 | tf_op jit(solution)/shard_map/psum | solution.py:31
  1038.8 3.7 copy-start.3
  1215.6 91.4 %collective-permute-start = (f32[16,256,256]{2,1,0:T(8,128)}, f32[16,256,256]{2,1,0:T(8,128)}, u32[]{:S(2)}, u32[]{:S(2)}) collective-permute-start(f32[16,256,256]{2,1,0:T(8,128)} %all-reduce.7.cloned.1.call-done), channel_id=1, source_target_pairs={{0,8},{8,16},{16,24},{24,0},{1,9},{9,17},{17,25},{25,1},{2,10},{10... | collective-permute-start | bytes 12582920 | tf_op jit(solution)/shard_map/ppermute | solution.py:20
  1215.6 97.2 %collective-permute-start.2 = (f32[16,256,256]{2,1,0:T(8,128)}, f32[16,256,256]{2,1,0:T(8,128)}, u32[]{:S(2)}, u32[]{:S(2)}) collective-permute-start(f32[16,256,256]{2,1,0:T(8,128)} %all-reduce.7.cloned.1.call-done), channel_id=1, source_target_pairs={{8,0},{16,8},{24,16},{0,24},{9,1},{17,9},{25,17},{1,25},{10,2},{18... | collective-permute-start | bytes 12582920 | tf_op jit(solution)/shard_map/ppermute | solution.py:22
  1306.9 48.2 %collective-permute-start.1 = (f32[16,256,256]{2,1,0:T(8,128)}, f32[16,256,256]{2,1,0:T(8,128)}, u32[]{:S(2)}, u32[]{:S(2)}) collective-permute-start(f32[16,256,256]{2,1,0:T(8,128)} %collective-permute-done), channel_id=1, source_target_pairs={{0,8},{8,16},{16,24},{24,0},{1,9},{9,17},{17,25},{25,1},{2,10},{10... | collective-permute-start | bytes 12582920 | tf_op jit(solution)/shard_map/ppermute | solution.py:20
  1307.0 5.6 copy-start.6
  1383.3 11.8 copy-start.4
  1395.1 34.9 %copy-start.2 = (f32[16,256,1,256]{1,3,2,0:T(8,128)S(1)}, f32[16,256,1,256]{1,3,2,0:T(8,128)}, u32[]{:S(2)}) copy-start(f32[16,256,1,256]{1,3,2,0:T(8,128)} %copy.83) | copy-start | bytes 12582916
  1430.0 4.8 copy-start.7
  1457.8 78.3 %copy-start.1 = (f32[1,1,8,256,256]{4,3,2,1,0:T(8,128)S(1)}, f32[1,1,8,256,256]{4,3,2,1,0:T(8,128)}, u32[]{:S(2)}) copy-start(f32[1,1,8,256,256]{4,3,2,1,0:T(8,128)} %param.10) | copy-start | bytes 6291460
Sparse Core Ops, SparseCore 0:
  983.8 30.4 all-reduce.4
  1059.2 156.3 all-reduce.6
